TPU v7x, 32 devices: a whole 2x2x4 slice. The times are simulated.
32 devices in a mesh: replica: 8 (over z, y), shard: 4 (over x, core).
Axes of the slice: x: 2, y: 2, z: 4, core: 2. Of those that a mesh axis runs over, the one named last changes fastest.
Arguments:
- hidden_in: bfloat16 [4096, 1024], P(('replica', 'shard')), may hold values from -6 to 6
- out_grad: bfloat16 [4096, 1024], P(('replica', 'shard')), may hold values from -6 to 6
- lengths: int32 [32, 4], P(('replica', 'shard')), may hold values from 1 to 64, 128 in all within a row
- norm1_gain: bfloat16 [1024], P('shard'), may hold values from 0.099609375 to 1.8984375
- norm1_bias: bfloat16 [1024], P('shard'), may hold values from -3 to 3
- qkv_weight: bfloat16 [1024, 3072], P('shard'), may hold values from -0.1875 to 0.1875
- query_bias: bfloat16 [1024], P('shard'), may hold values from -3 to 3
- value_bias: bfloat16 [1024], P('shard'), may hold values from -3 to 3
- out_weight: bfloat16 [1024, 1024], P('shard'), may hold values from -0.75 to 0.75
- out_bias: bfloat16 [1024], P('shard'), may hold values from -3 to 3
- norm2_gain: bfloat16 [1024], P('shard'), may hold values from 0.099609375 to 1.8984375
- norm2_bias: bfloat16 [1024], P('shard'), may hold values from -3 to 3
- up_weight: bfloat16 [1024, 4096], P('shard'), may hold values from -0.1875 to 0.1875
- up_bias: bfloat16 [4096], P('shard'), may hold values from -3 to 3
- down_weight: bfloat16 [4096, 1024], P('shard'), may hold values from -0.125 to 0.125
- down_bias: bfloat16 [1024], P('shard'), may hold values from -3 to 3
Outputs:
- hidden_out: bfloat16 [4096, 1024], P(('replica', 'shard'))
- in_grad: bfloat16 [4096, 1024], P(('replica', 'shard'))
- norm1_gain_grad: float32 [1024], P('shard')
- norm1_bias_grad: float32 [1024], P('shard')
- qkv_weight_grad: float32 [1024, 3072], P('shard')
- query_bias_grad: float32 [1024], P('shard')
- value_bias_grad: float32 [1024], P('shard')
- out_weight_grad: float32 [1024, 1024], P('shard')
- out_bias_grad: float32 [1024], P('shard')
- norm2_gain_grad: float32 [1024], P('shard')
- norm2_bias_grad: float32 [1024], P('shard')
- up_weight_grad: float32 [1024, 4096], P('shard')
- up_bias_grad: float32 [4096], P('shard')
- down_weight_grad: float32 [4096, 1024], P('shard')
- down_bias_grad: float32 [1024], P('shard')
Inputs may be any that keep to these rules, and one draw needn't show every extreme that they name: The 4 lengths of each device add up to 128, and the largest of all is 64.
All inputs are finite; a program needn't handle non-finite values.
Results may differ from a plain program's by a relative error of at most 0.018.
Values may be sent and summed in bfloat16 or wider, within the bound.
A program may use at most 192 MiB of HBM per device.

v0:
```python
import math
import jax
import jax.numpy as jnp
from jax import lax
from jax.sharding import PartitionSpec as P

HEADS = 16
HEAD_DIM = 64
EPSILON = 1e-05
TANH_SCALE = math.sqrt(2.0 / math.pi)
CUBIC = 0.044715


def product(left, right):
    return jnp.dot(left, right, preferred_element_type=jnp.float32)


def left_product(left, right):
    return lax.dot_general(
        left, right, (((0,), (0,)), ((), ())), preferred_element_type=jnp.float32
    )


def right_product(left, right):
    return lax.dot_general(
        left, right, (((1,), (1,)), ((), ())), preferred_element_type=jnp.float32
    )


def column_term(left, right):
    return left_product(left, right)


def gelu_parts(pre_act):
    inner_arg = TANH_SCALE * (pre_act + CUBIC * pre_act * pre_act * pre_act)
    tangent = jnp.tanh(inner_arg)
    gelu_value = 0.5 * pre_act * (1.0 + tangent)
    gelu_slope = 0.5 * (1.0 + tangent) + 0.5 * pre_act * (1.0 - tangent * tangent) * TANH_SCALE * (
        1.0 + 3.0 * CUBIC * pre_act * pre_act
    )
    return (gelu_value, gelu_slope)


def layer_norm(inputs, gain_row, bias_row):
    average = jnp.mean(inputs, axis=-1, keepdims=True)
    centred = inputs - average
    inv_std = lax.rsqrt(jnp.mean(centred * centred, axis=-1, keepdims=True) + EPSILON)
    normed = centred * inv_std
    return (normed * gain_row.astype(jnp.float32) + bias_row.astype(jnp.float32), normed, inv_std)


def norm_back(upstream, normed, inv_std, gain_row):
    scaled = upstream * gain_row.astype(jnp.float32)
    first_term = jnp.mean(scaled, axis=-1, keepdims=True)
    second_term = jnp.mean(scaled * normed, axis=-1, keepdims=True)
    input_grad = inv_std * (scaled - first_term - normed * second_term)
    return (input_grad, jnp.sum(upstream * normed, axis=0), jnp.sum(upstream, axis=0))


def seq_mask(lengths, row_count):
    seq_ends = jnp.cumsum(lengths, axis=-1)
    places = jnp.arange(row_count, dtype=jnp.int32)
    segment = jnp.sum((places[None, :, None] >= seq_ends[:, None, :]).astype(jnp.int32), axis=-1)
    causal = places[None, :] <= places[:, None]
    return (segment[:, :, None] == segment[:, None, :]) & causal[None]


def split_heads(flat_rows, groups):
    return flat_rows.reshape(groups, -1, HEADS, HEAD_DIM)


def attend_forward(queries, key_rows, values, allowed):
    groups = allowed.shape[0]
    scale_factor = 1.0 / math.sqrt(HEAD_DIM)
    head_q = split_heads(queries, groups)
    head_k = split_heads(key_rows, groups)
    head_v = split_heads(values, groups)
    scores = (
        jnp.einsum("gqhd,gkhd->ghqk", head_q, head_k, preferred_element_type=jnp.float32)
        * scale_factor
    )
    visible = allowed[:, None]
    row_total = jnp.sum(jnp.where(visible, jnp.exp(scores), 0.0), axis=-1, keepdims=True)
    log_total = jnp.log(row_total)
    probs_round = jnp.where(visible, jnp.exp(scores - log_total), 0.0).astype(jnp.bfloat16)
    context = jnp.einsum("ghqk,gkhd->gqhd", probs_round, head_v, preferred_element_type=jnp.float32)
    return (context.reshape(-1, HEADS * HEAD_DIM).astype(jnp.bfloat16), log_total)


def attend_backward(queries, key_rows, values, allowed, log_total, context_grad):
    groups = allowed.shape[0]
    scale_factor = 1.0 / math.sqrt(HEAD_DIM)
    head_q = split_heads(queries, groups)
    head_k = split_heads(key_rows, groups)
    head_v = split_heads(values, groups)
    head_g = split_heads(context_grad, groups)
    scores = (
        jnp.einsum("gqhd,gkhd->ghqk", head_q, head_k, preferred_element_type=jnp.float32)
        * scale_factor
    )
    visible = allowed[:, None]
    exact_probs = jnp.where(visible, jnp.exp(scores - log_total), 0.0)
    probs_round = exact_probs.astype(jnp.bfloat16)
    prob_grad = jnp.einsum("gqhd,gkhd->ghqk", head_g, head_v, preferred_element_type=jnp.float32)
    value_grad = jnp.einsum(
        "ghqk,gqhd->gkhd", probs_round, head_g, preferred_element_type=jnp.float32
    )
    row_delta = jnp.sum(exact_probs * prob_grad, axis=-1, keepdims=True)
    score_grad = (exact_probs * (prob_grad - row_delta) * scale_factor).astype(jnp.bfloat16)
    query_grad = jnp.einsum(
        "ghqk,gkhd->gqhd", score_grad, head_k, preferred_element_type=jnp.float32
    )
    key_grad = jnp.einsum("ghqk,gqhd->gkhd", score_grad, head_q, preferred_element_type=jnp.float32)
    model_width = HEADS * HEAD_DIM
    return (
        query_grad.reshape(-1, model_width),
        key_grad.reshape(-1, model_width),
        value_grad.reshape(-1, model_width),
    )


def local(
    hidden_in,
    out_grad,
    lengths,
    norm1_gain,
    norm1_bias,
    qkv_weight,
    query_bias,
    value_bias,
    out_weight,
    out_bias,
    norm2_gain,
    norm2_bias,
    up_weight,
    up_bias,
    down_weight,
    down_bias,
):
    (
        gain_one,
        bias_one,
        qkv_full,
        qbias_full,
        vbias_full,
        outw_full,
        outb_full,
        gain_two,
        bias_two,
        upw_full,
        upb_full,
        downw_full,
        downb_full,
    ) = (
        lax.all_gather(norm1_gain, "shard", axis=0, tiled=True),
        lax.all_gather(norm1_bias, "shard", axis=0, tiled=True),
        lax.all_gather(qkv_weight, "shard", axis=0, tiled=True),
        lax.all_gather(query_bias, "shard", axis=0, tiled=True),
        lax.all_gather(value_bias, "shard", axis=0, tiled=True),
        lax.all_gather(out_weight, "shard", axis=0, tiled=True),
        lax.all_gather(out_bias, "shard", axis=0, tiled=True),
        lax.all_gather(norm2_gain, "shard", axis=0, tiled=True),
        lax.all_gather(norm2_bias, "shard", axis=0, tiled=True),
        lax.all_gather(up_weight, "shard", axis=0, tiled=True),
        lax.all_gather(up_bias, "shard", axis=0, tiled=True),
        lax.all_gather(down_weight, "shard", axis=0, tiled=True),
        lax.all_gather(down_bias, "shard", axis=0, tiled=True),
    )
    allowed = seq_mask(lengths, hidden_in.shape[0])
    model_width = hidden_in.shape[1]
    inputs_wide = hidden_in.astype(jnp.float32)
    first_out, normed_one, inv_one = layer_norm(inputs_wide, gain_one, bias_one)
    first_in = first_out.astype(jnp.bfloat16)
    projected = product(first_in, qkv_full)
    queries = (projected[:, :model_width] + qbias_full.astype(jnp.float32)).astype(jnp.bfloat16)
    key_rows = projected[:, model_width : 2 * model_width].astype(jnp.bfloat16)
    values = (projected[:, 2 * model_width :] + vbias_full.astype(jnp.float32)).astype(jnp.bfloat16)
    context, log_total = attend_forward(queries, key_rows, values, allowed)
    residual = inputs_wide + product(context, outw_full) + outb_full.astype(jnp.float32)
    second_out, normed_two, inv_two = layer_norm(residual, gain_two, bias_two)
    second_in = second_out.astype(jnp.bfloat16)
    pre_act = product(second_in, upw_full) + upb_full.astype(jnp.float32)
    activ_value, gelu_slope = gelu_parts(pre_act)
    activated = activ_value.astype(jnp.bfloat16)
    hidden_out = (
        residual + product(activated, downw_full) + downb_full.astype(jnp.float32)
    ).astype(jnp.bfloat16)
    back_qkv, back_out, back_up, back_down, back_gain1, back_gain2 = (
        qkv_full,
        outw_full,
        upw_full,
        downw_full,
        gain_one,
        gain_two,
    )
    upstream = out_grad.astype(jnp.float32)
    down_owned = lax.psum_scatter(
        column_term(activated, out_grad).astype(jnp.bfloat16),
        "shard",
        scatter_dimension=0,
        tiled=True,
    )
    down_bgrad = jnp.sum(upstream, axis=0)
    pre_grad = right_product(out_grad, back_down) * gelu_slope
    pre_round = pre_grad.astype(jnp.bfloat16)
    up_bgrad = jnp.sum(pre_grad, axis=0)
    up_owned = lax.psum_scatter(
        column_term(second_in, pre_round).astype(jnp.bfloat16),
        "shard",
        scatter_dimension=0,
        tiled=True,
    )
    second_grad = right_product(pre_round, back_up)
    norm_two_in, gain2_grad, bias2_grad = norm_back(second_grad, normed_two, inv_two, back_gain2)
    resid_grad = upstream + norm_two_in
    resid_round = resid_grad.astype(jnp.bfloat16)
    out_bgrad = jnp.sum(resid_grad, axis=0)
    out_owned = lax.psum_scatter(
        column_term(context, resid_round).astype(jnp.bfloat16),
        "shard",
        scatter_dimension=0,
        tiled=True,
    )
    context_grad = right_product(resid_round, back_out).astype(jnp.bfloat16)
    query_grad, key_grad, value_grad = attend_backward(
        queries, key_rows, values, allowed, log_total, context_grad
    )
    query_bgrad = jnp.sum(query_grad, axis=0)
    value_bgrad = jnp.sum(value_grad, axis=0)
    qkv_grad = jnp.concatenate([query_grad, key_grad, value_grad], axis=1).astype(jnp.bfloat16)
    qkv_owned = lax.psum_scatter(
        column_term(first_in, qkv_grad).astype(jnp.bfloat16),
        "shard",
        scatter_dimension=0,
        tiled=True,
    )
    first_grad = right_product(qkv_grad, back_qkv)
    norm_one_in, gain1_grad, bias1_grad = norm_back(first_grad, normed_one, inv_one, back_gain1)
    in_grad = (resid_grad + norm_one_in).astype(jnp.bfloat16)
    (
        gain1_own,
        bias1_own,
        qbias_own,
        vbias_own,
        outb_own,
        gain2_own,
        bias2_own,
        upb_own,
        downb_own,
    ) = (
        lax.psum_scatter(
            gain1_grad.astype(jnp.bfloat16), "shard", scatter_dimension=0, tiled=True
        ).astype(jnp.float32),
        lax.psum_scatter(
            bias1_grad.astype(jnp.bfloat16), "shard", scatter_dimension=0, tiled=True
        ).astype(jnp.float32),
        lax.psum_scatter(
            query_bgrad.astype(jnp.bfloat16), "shard", scatter_dimension=0, tiled=True
        ).astype(jnp.float32),
        lax.psum_scatter(
            value_bgrad.astype(jnp.bfloat16), "shard", scatter_dimension=0, tiled=True
        ).astype(jnp.float32),
        lax.psum_scatter(
            out_bgrad.astype(jnp.bfloat16), "shard", scatter_dimension=0, tiled=True
        ).astype(jnp.float32),
        lax.psum_scatter(
            gain2_grad.astype(jnp.bfloat16), "shard", scatter_dimension=0, tiled=True
        ).astype(jnp.float32),
        lax.psum_scatter(
            bias2_grad.astype(jnp.bfloat16), "shard", scatter_dimension=0, tiled=True
        ).astype(jnp.float32),
        lax.psum_scatter(
            up_bgrad.astype(jnp.bfloat16), "shard", scatter_dimension=0, tiled=True
        ).astype(jnp.float32),
        lax.psum_scatter(
            down_bgrad.astype(jnp.bfloat16), "shard", scatter_dimension=0, tiled=True
        ).astype(jnp.float32),
    )
    (
        gain1_total,
        bias1_total,
        qkv_total,
        qbias_total,
        vbias_total,
        outw_total,
        outb_total,
        gain2_total,
        bias2_total,
        upw_total,
        upb_total,
        downw_total,
        downb_total,
    ) = (
        lax.psum(gain1_own.astype(jnp.bfloat16), "replica").astype(jnp.float32),
        lax.psum(bias1_own.astype(jnp.bfloat16), "replica").astype(jnp.float32),
        lax.psum(qkv_owned, "replica").astype(jnp.float32),
        lax.psum(qbias_own.astype(jnp.bfloat16), "replica").astype(jnp.float32),
        lax.psum(vbias_own.astype(jnp.bfloat16), "replica").astype(jnp.float32),
        lax.psum(out_owned, "replica").astype(jnp.float32),
        lax.psum(outb_own.astype(jnp.bfloat16), "replica").astype(jnp.float32),
        lax.psum(gain2_own.astype(jnp.bfloat16), "replica").astype(jnp.float32),
        lax.psum(bias2_own.astype(jnp.bfloat16), "replica").astype(jnp.float32),
        lax.psum(up_owned, "replica").astype(jnp.float32),
        lax.psum(upb_own.astype(jnp.bfloat16), "replica").astype(jnp.float32),
        lax.psum(down_owned, "replica").astype(jnp.float32),
        lax.psum(downb_own.astype(jnp.bfloat16), "replica").astype(jnp.float32),
    )
    return (
        hidden_out,
        in_grad,
        gain1_total,
        bias1_total,
        qkv_total,
        qbias_total,
        vbias_total,
        outw_total,
        outb_total,
        gain2_total,
        bias2_total,
        upw_total,
        upb_total,
        downw_total,
        downb_total,
    )


def solution(mesh):
    in_specs = (
        P(("replica", "shard"), None),
        P(("replica", "shard"), None),
        P(("replica", "shard"), None),
        P("shard"),
        P("shard"),
        P("shard", None),
        P("shard"),
        P("shard"),
        P("shard", None),
        P("shard"),
        P("shard"),
        P("shard"),
        P("shard", None),
        P("shard"),
        P("shard", None),
        P("shard"),
    )
    out_specs = (
        P(("replica", "shard"), None),
        P(("replica", "shard"), None),
        P("shard"),
        P("shard"),
        P("shard", None),
        P("shard"),
        P("shard"),
        P("shard", None),
        P("shard"),
        P("shard"),
        P("shard"),
        P("shard", None),
        P("shard"),
        P("shard", None),
        P("shard"),
    )
    return jax.shard_map(local, mesh=mesh, in_specs=in_specs, out_specs=out_specs, check_vma=False)
```

profile of v0, /device:TPU:0, one launch (start us, length us, event | category | flops | bytes accessed | tf_op | source)
XLA Modules:
  0.0 687.5 jit_solution(8565300499013674690)
XLA Ops:
  10.1 6.0 all-gather.4
  16.2 5.4 all-gather.1
  21.6 5.2 all-gather
  26.8 5.2 all-gather.3
  32.0 5.2 all-gather.2
  37.3 5.4 all_gather.49
  42.6 5.2 all-gather.6
  47.9 5.2 all-gather.5
  53.8 5.0 all-gather.13.cloned.1.call-done
  58.8 3.9 fusion.66
  64.3 18.7 %all-gather.15.cloned.1.call-done = bf16[1024,1024]{1,0:T(8,128)(2,1)} async-done(((bf16[256,1024]{1,0:T(8,128)(2,1)}), bf16[1024,1024]{1,0:T(8,128)(2,1)}) %all-gather.15.cloned.1.call-update) | async-done | bytes 2097168 | tf_op jit(solution)/shard_map/all_gather | solution.py:160
  85.4 57.5 %all-gather.17.cloned.1.call-done = bf16[1024,4096]{1,0:T(8,128)(2,1)} async-done(((bf16[256,4096]{1,0:T(8,128)(2,1)}), bf16[1024,4096]{1,0:T(8,128)(2,1)}) %all-gather.17.cloned.1.call-update) | async-done | bytes 8388624 | tf_op jit(solution)/shard_map/all_gather | solution.py:164
  142.8 4.8 convolution_add_fusion
  147.6 54.9 %all-gather.19.cloned.1.call-done = bf16[4096,1024]{1,0:T(8,128)(2,1)} async-done(((bf16[1024,1024]{1,0:T(8,128)(2,1)}), bf16[4096,1024]{1,0:T(8,128)(2,1)}) %all-gather.19.cloned.1.call-update) | async-done | bytes 8388624 | tf_op jit(solution)/shard_map/all_gather | solution.py:166
  202.5 7.1 %fusion.74 = (bf16[4096]{0:T(1024)(128)(2,1)S(1)}, bf16[128,4096]{1,0:T(8,128)(2,1)S(1)}) fusion(f32[128,4096]{1,0:T(8,128)S(1)} %convolution_add_fusion, bf16[128,1024]{1,0:T(8,128)(2,1)S(1)} %copy-done.4, bf16[4096,1024]{1,0:T(8,128)(2,1)} %all-gather.19.cloned.1.call-done), kind=kOutput, calls=%fused_computation.108 | convolution fusion | flops 1084223488 | bytes 11804672 | tf_op jit(solution)/shard_map/dot_general | solution.py:25
  209.6 3.0 multiply_reduce_fusion.1
  221.7 3.2 fusion.69
  227.2 3.6 convolution_convert_fusion.4
  230.8 3.7 fusion.70
  234.5 5.8 convolution_convert_fusion.2
  240.4 6.9 %convolution_convert_fusion.1 = bf16[1024,4096]{1,0:T(8,128)(2,1)} fusion(bf16[128,4096]{1,0:T(8,128)(2,1)} %copy-done.3, f32[128,1024]{1,0:T(8,128)S(1)} %get-tuple-element.54, f32[1024]{0:T(1024)S(1)} %bitcast.77, f32[1024]{0:T(1024)S(1)} %bitcast.69, f32[128]{0:T(128)S(1)} %add_rsqrt_fusion, f32[128]{0:T(128)S(1)} %broadcast_multiply_fusion.4), kind=kOutput, calls=%fused_computation.3 | convolution fusion | flops 1078591488 | bytes 9970688 | tf_op jit(solution)/shard_map/dot_general | solution.py:19
  247.3 6.6 convolution_convert_fusion
  254.0 53.6 %reduce-scatter.5.cloned.1.call-done = bf16[256,3072]{1,0:T(8,128)(2,1)} async-done(((bf16[1024,3072]{1,0:T(8,128)(2,1)}), bf16[256,3072]{1,0:T(8,128)(2,1)}) %reduce-scatter.5.cloned.1.call-update) | async-done | bytes 1572880 | tf_op jit(solution)/shard_map/reduce_scatter | solution.py:231
  307.6 74.0 %reduce-scatter.9.cloned.1.call-done = bf16[256,4096]{1,0:T(8,128)(2,1)} async-done(((bf16[1024,4096]{1,0:T(8,128)(2,1)}), bf16[256,4096]{1,0:T(8,128)(2,1)}) %reduce-scatter.9.cloned.1.call-update) | async-done | bytes 2097168 | tf_op jit(solution)/shard_map/reduce_scatter | solution.py:207
  381.6 74.0 %reduce-scatter.11.cloned.1.call-done = bf16[1024,1024]{1,0:T(8,128)(2,1)} async-done(((bf16[4096,1024]{1,0:T(8,128)(2,1)}), bf16[1024,1024]{1,0:T(8,128)(2,1)}) %reduce-scatter.11.cloned.1.call-update) | async-done | bytes 2097168 | tf_op jit(solution)/shard_map/reduce_scatter | solution.py:197
  456.3 5.1 all-gather.7
  464.4 6.9 fusion.37
  471.3 11.3 %all-reduce.11 = (bf16[1024]{0:T(1024)(128)(2,1)S(1)}, bf16[1024]{0:T(1024)(128)(2,1)S(1)}, bf16[1024]{0:T(1024)(128)(2,1)S(1)}, bf16[1024]{0:T(1024)(128)(2,1)S...) all-reduce(bf16[1024]{0:T(1024)(128)(2,1)S(1)} %get-tuple-element.1, ...), channel_id=2, replica_groups=mesh['replica'=8,'shard'=4] {'shard'}, use_global_device_ids=true, to_apply=%region_13.14.clone | all-reduce | flops 12288 | bytes 49152
  483.2 23.3 %all-reduce.9 = (bf16[256]{0:T(256)(128)(2,1)S(1)}, bf16[256]{0:T(256)(128)(2,1)S(1)}, bf16[256]{0:T(256)(128)(2,1)S(1)}, bf16[256]{0:T(256)(128)(2,1)S(1)}, bf1...) all-reduce(bf16[256]{0:T(256)(128)(2,1)S(1)} %dynamic-slice.1, ...), channel_id=1, replica_groups=mesh['replica'=8,'shard'=4] {'replica'}, use_global_device_ids=true, to_apply=%region_14.15 | all-reduce | flops 3072 | bytes 12288 | tf_op jit(solution)/shard_map/psum | solution.py:294
  513.6 5.6 fusion.17
  519.2 152.1 %all-reduce.14.cloned.1.call-done = (bf16[256,3072]{1,0:T(8,128)(2,1)}, bf16[256,1024]{1,0:T(8,128)(2,1)}, bf16[256,4096]{1,0:T(8,128)(2,1)}, bf16[1024,1024]{1,0:T(8,128)(2,1)}) async-done(((bf16[256,3072]{1,0:T(8,128)(2,1)}, bf16[256,1024]{1,0:T(8,128)(2,1)}, bf16[256,4096]{1,0:T(8,128)(2,1)}, bf16[1024,1024]{1,0:T(8,128)(2,1)}), (bf16[256,3072]{1,0:T(8,128)(2,1)}, bf16[256,1024]{1,0:T(8,128)(2,1)}, ...) | async-done | bytes 6291472 | tf_op jit(solution)/shard_map/psum | solution.py:296
  671.3 3.6 convert_element_type.232
  (141 shorter events, 35.1 us)
Async XLA Ops:
  7.2 51.6 %all-gather.13.cloned.1.call-start = ((), (), s32[]{:S(2)}) async-start(), calls=%async_computation.4 | async-start | bytes 7864320 | tf_op jit(solution)/shard_map/all_gather | solution.py:157
  7.9 75.1 %all-gather.15.cloned.1.call-start = ((), (), s32[]{:S(2)}) async-start(), calls=%async_computation.5 | async-start | bytes 2621440 | tf_op jit(solution)/shard_map/all_gather | solution.py:160
  8.7 7.5 %copy-start.17 = (bf16[256]{0:T(256)(128)(2,1)S(1)}, bf16[256]{0:T(256)(128)(2,1)}, u32[]{:S(2)}) copy-start(bf16[256]{0:T(256)(128)(2,1)} %param.20) | copy-start | bytes 1540
  8.7 12.9 %copy-start.18 = (bf16[256]{0:T(256)(128)(2,1)S(1)}, bf16[256]{0:T(256)(128)(2,1)}, u32[]{:S(2)}) copy-start(bf16[256]{0:T(256)(128)(2,1)} %param.19) | copy-start | bytes 1540
  8.7 18.1 %copy-start.19 = (bf16[256]{0:T(256)(128)(2,1)S(1)}, bf16[256]{0:T(256)(128)(2,1)}, u32[]{:S(2)}) copy-start(bf16[256]{0:T(256)(128)(2,1)} %param.22) | copy-start | bytes 1540
  8.7 23.3 %copy-start.20 = (bf16[256]{0:T(256)(128)(2,1)S(1)}, bf16[256]{0:T(256)(128)(2,1)}, u32[]{:S(2)}) copy-start(bf16[256]{0:T(256)(128)(2,1)} %param.23) | copy-start | bytes 1540
  8.7 28.5 %copy-start.15 = (bf16[1024]{0:T(1024)(128)(2,1)S(1)}, bf16[1024]{0:T(1024)(128)(2,1)}, u32[]{:S(2)}) copy-start(bf16[1024]{0:T(1024)(128)(2,1)} %param.29) | copy-start | bytes 6148
  8.7 33.9 %copy-start.21 = (bf16[256]{0:T(256)(128)(2,1)S(1)}, bf16[256]{0:T(256)(128)(2,1)}, u32[]{:S(2)}) copy-start(bf16[256]{0:T(256)(128)(2,1)} %param.27) | copy-start | bytes 1540
  8.7 39.1 %copy-start.22 = (bf16[256]{0:T(256)(128)(2,1)S(1)}, bf16[256]{0:T(256)(128)(2,1)}, u32[]{:S(2)}) copy-start(bf16[256]{0:T(256)(128)(2,1)} %param.26) | copy-start | bytes 1540
  8.7 44.3 %copy-start.23 = (s32[1,4]{1,0:T(1,128)S(1)}, s32[1,4]{1,0:T(1,128)}, u32[]{:S(2)}) copy-start(s32[1,4]{1,0:T(1,128)} %param.18) | copy-start | bytes 52
  8.8 44.6 %copy-start.1 = (bf16[128,1024]{1,0:T(8,128)(2,1)S(1)}, bf16[128,1024]{1,0:T(8,128)(2,1)}, u32[]{:S(2)}) copy-start(bf16[128,1024]{1,0:T(8,128)(2,1)} %param.16) | copy-start | bytes 786436
  8.8 134.1 %all-gather.17.cloned.1.call-start = ((), (), s32[]{:S(2)}) async-start(), calls=%async_computation.6 | async-start | bytes 10485760 | tf_op jit(solution)/shard_map/all_gather | solution.py:164
  9.5 193.0 %all-gather.19.cloned.1.call-start = ((), (), s32[]{:S(2)}) async-start(), calls=%async_computation.7 | async-start | bytes 10485760 | tf_op jit(solution)/shard_map/all_gather | solution.py:166
  10.1 243.9 %reduce-scatter.7.cloned.1.call-start = ((), (), s32[]{:S(2)}) async-start(), calls=%async_computation.9 | async-start | bytes 2621440 | tf_op jit(solution)/shard_map/reduce_scatter | solution.py:218
  63.2 21.9 %copy-start.11 = (bf16[128,1024]{0,1:T(8,128)(2,1)}, bf16[128,1024]{0,1:T(8,128)(2,1)S(1)}, u32[]{:S(2)}) copy-start(bf16[128,1024]{0,1:T(8,128)(2,1)S(1)} %copy.60) | copy-start | bytes 786436
  63.4 21.7 %copy-start.9 = (bf16[128,1024]{0,1:T(8,128)(2,1)}, bf16[128,1024]{0,1:T(8,128)(2,1)S(1)}, u32[]{:S(2)}) copy-start(bf16[128,1024]{0,1:T(8,128)(2,1)S(1)} %copy.61) | copy-start | bytes 786436
  63.8 19.2 %copy-start.8 = (f32[16,128,128]{1,2,0:T(8,128)}, f32[16,128,128]{1,2,0:T(8,128)S(1)}, u32[]{:S(2)}) copy-start(f32[16,128,128]{1,2,0:T(8,128)S(1)} %convolution_multiply_fusion.1) | copy-start | bytes 3145732
  64.3 78.6 %copy-start.12 = (bf16[16,64,128]{2,1,0:T(8,128)(2,1)}, bf16[16,64,128]{2,1,0:T(8,128)(2,1)S(1)}, u32[]{:S(2)}) copy-start(bf16[16,64,128]{2,1,0:T(8,128)(2,1)S(1)} %convolution_convert_fusion.6) | copy-start | bytes 786436
  142.8 59.7 %copy-start.4 = (bf16[128,1024]{1,0:T(8,128)(2,1)S(1)}, bf16[128,1024]{1,0:T(8,128)(2,1)}, u32[]{:S(2)}) copy-start(bf16[128,1024]{1,0:T(8,128)(2,1)} %param.17) | copy-start | bytes 786436
  202.5 7.1 %copy-start = (bf16[1024,4096]{1,0:T(8,128)(2,1)S(1)}, bf16[1024,4096]{1,0:T(8,128)(2,1)}, u32[]{:S(2)}) copy-start(bf16[1024,4096]{1,0:T(8,128)(2,1)} %all-gather.17.cloned.1.call-done) | copy-start | bytes 25165828
  209.6 3.1 copy-start.3
  209.6 3.1 copy-start.5
  209.6 3.3 copy-start.13
  215.0 92.6 %reduce-scatter.5.cloned.1.call-start = ((), (), s32[]{:S(2)}) async-start(), calls=%async_computation.8 | async-start | bytes 7864320 | tf_op jit(solution)/shard_map/reduce_scatter | solution.py:231
  215.2 3.0 copy-start.2
  240.3 141.3 %reduce-scatter.9.cloned.1.call-start = ((), (), s32[]{:S(2)}) async-start(), calls=%async_computation.10 | async-start | bytes 10485760 | tf_op jit(solution)/shard_map/reduce_scatter | solution.py:207
  247.3 208.4 %reduce-scatter.11.cloned.1.call-start = ((), (), s32[]{:S(2)}) async-start(), calls=%async_computation.11 | async-start | bytes 10485760 | tf_op jit(solution)/shard_map/reduce_scatter | solution.py:197
  253.9 417.3 %all-reduce.14.cloned.1.call-start = ((), (), s32[]{:S(2)}) async-start(), calls=%async_computation.12 | async-start | bytes 12582912 | tf_op jit(solution)/shard_map/psum | solution.py:296
  455.7 6.7 copy-start.25
  671.3 3.6 copy-start.14
  671.3 4.7 copy-start.7
  676.0 2.5 copy-start.6
  (3 other events, 3.3 us)
Sparse Core Ops, SparseCore 0:
  9.6 49.2 all-gather.12
  60.4 22.5 all-gather.14
  84.5 58.2 all-gather.16
  144.2 58.2 all-gather.18
  215.1 31.1 reduce-scatter.6
  248.7 58.8 reduce-scatter.4
  310.2 71.3 reduce-scatter.8
  384.2 71.4 reduce-scatter.10
  460.1 211.1 all-reduce.13
where the time goes:
time: 688 us; the launch traced here: 687 us
  waiting for transfers between devices  493 us (72%)
  blocking collectives  82.4 us (12%)
  matrix products  69.8 us (10%)
  other arithmetic  22.1 us (3%)
  between operations  15.6 us (2%)
    psum x1, waiting for transfers between devices, local(): lax.psum(qkv_owned, 'replica').astype(jnp.float32)  152 us
    reduce_scatter x1, waiting for transfers between devices, local(): lax.psum_scatter(column_term(activated, out_grad).astype(jnp.bfloat16), '...  74 us
    reduce_scatter x1, waiting for transfers between devices, local(): lax.psum_scatter(column_term(second_in, pre_round).astype(jnp.bfloat16),...  74 us
    all_gather x1, waiting for transfers between devices, local(): lax.all_gather(up_weight, 'shard', axis=0, tiled=True)  57.5 us
    all_gather x1, waiting for transfers between devices, local(): lax.all_gather(down_weight, 'shard', axis=0, tiled=True)  54.9 us
    reduce_scatter x1, waiting for transfers between devices, local(): lax.psum_scatter(column_term(first_in, qkv_grad).astype(jnp.bfloat16), 's...  53.6 us
    psum x1, blocking collectives, local(): lax.psum(gain1_own.astype(jnp.bfloat16), 'replica').astype(jnp.float32)  23.3 us
    dot_general x4, matrix products, left_product(): lax.dot_general(left, right, (((0,), (0,)), ((), ())), preferred_element_...  21.3 us
  transfers between devices with their start and end apart: 9, of which 8 were waited for; matrix products, arithmetic and copies ran while one was open for 11% of the time, Pallas kernels for 0%

commit v1 on v0

--- a/solution.py
+++ b/solution.py
@@ -293,7 +293,7 @@
     ) = (
         lax.psum(gain1_own.astype(jnp.bfloat16), "replica").astype(jnp.float32),
         lax.psum(bias1_own.astype(jnp.bfloat16), "replica").astype(jnp.float32),
-        lax.psum(qkv_owned, "replica").astype(jnp.float32),
+        jnp.sum(lax.all_gather(qkv_owned, "replica"), axis=0).astype(jnp.float32),
         lax.psum(qbias_own.astype(jnp.bfloat16), "replica").astype(jnp.float32),
         lax.psum(vbias_own.astype(jnp.bfloat16), "replica").astype(jnp.float32),
         lax.psum(out_owned, "replica").astype(jnp.float32),

time: 688 us -> 824 us (1.20)
  waiting for transfers between devices: 493 us -> 620 us
  other arithmetic: 22.1 us -> 30.6 us
    all_gather x0 -> x1, waiting for transfers between devices: none -> 168 us  [local(): lax.all_gather(qkv_owned, 'replica')]
    psum x1, waiting for transfers between devices: 152 us -> 111 us  [local(): lax.psum(out_owned, 'replica').astype(jnp.float32)]
  transfers between devices with their start and end apart: 9 -> 10, of which waited for: 8 -> 9; matrix products, arithmetic and copies ran while one was open for 11% -> 10% of each run, Pallas kernels for 0% -> 0%
where the time goes in v1:
time: 824 us; the launch traced here: 823 us
  waiting for transfers between devices  620 us (75%)
  blocking collectives  82.3 us (10%)
  matrix products  69.9 us (8%)
  other arithmetic  30.6 us (4%)
  between operations  15.9 us (2%)
    all_gather x1, waiting for transfers between devices, local(): lax.all_gather(qkv_owned, 'replica')  168 us
    psum x1, waiting for transfers between devices, local(): lax.psum(out_owned, 'replica').astype(jnp.float32)  111 us
    reduce_scatter x1, waiting for transfers between devices, local(): lax.psum_scatter(column_term(activated, out_grad).astype(jnp.bfloat16), '...  74 us
    reduce_scatter x1, waiting for transfers between devices, local(): lax.psum_scatter(column_term(second_in, pre_round).astype(jnp.bfloat16),...  66.5 us
    reduce_scatter x1, waiting for transfers between devices, local(): lax.psum_scatter(column_term(first_in, qkv_grad).astype(jnp.bfloat16), 's...  61.3 us
    all_gather x1, waiting for transfers between devices, local(): lax.all_gather(up_weight, 'shard', axis=0, tiled=True)  57.5 us
    all_gather x1, waiting for transfers between devices, local(): lax.all_gather(down_weight, 'shard', axis=0, tiled=True)  54.9 us
    psum x1, blocking collectives, local(): lax.psum(gain1_own.astype(jnp.bfloat16), 'replica').astype(jnp.float32)  23.1 us
  transfers between devices with their start and end apart: 10, of which 9 were waited for; matrix products, arithmetic and copies ran while one was open for 10% of the time, Pallas kernels for 0%

profile of v1, /device:TPU:0, one launch (start us, length us, event | category | flops | bytes accessed | tf_op | source)
XLA Modules:
  0.0 823.2 jit_solution(16255423062943975380)
XLA Ops:
  10.1 6.0 all-gather.5
  16.2 5.4 all-gather.2
  21.6 5.2 all-gather.1
  26.8 5.2 all-gather.4
  32.0 5.2 all-gather.3
  37.3 5.4 all_gather.55
  42.6 5.2 all-gather.7
  47.9 5.2 all-gather.6
  53.8 5.0 all-gather.15.cloned.1.call-done
  58.8 3.9 fusion.66
  64.3 18.7 %all-gather.17.cloned.1.call-done = bf16[1024,1024]{1,0:T(8,128)(2,1)} async-done(((bf16[256,1024]{1,0:T(8,128)(2,1)}), bf16[1024,1024]{1,0:T(8,128)(2,1)}) %all-gather.17.cloned.1.call-update) | async-done | bytes 2097168 | tf_op jit(solution)/shard_map/all_gather | solution.py:160
  85.4 57.5 %all-gather.19.cloned.1.call-done = bf16[1024,4096]{1,0:T(8,128)(2,1)} async-done(((bf16[256,4096]{1,0:T(8,128)(2,1)}), bf16[1024,4096]{1,0:T(8,128)(2,1)}) %all-gather.19.cloned.1.call-update) | async-done | bytes 8388624 | tf_op jit(solution)/shard_map/all_gather | solution.py:164
  142.8 4.8 convolution_add_fusion
  147.6 54.9 %all-gather.21.cloned.1.call-done = bf16[4096,1024]{1,0:T(8,128)(2,1)} async-done(((bf16[1024,1024]{1,0:T(8,128)(2,1)}), bf16[4096,1024]{1,0:T(8,128)(2,1)}) %all-gather.21.cloned.1.call-update) | async-done | bytes 8388624 | tf_op jit(solution)/shard_map/all_gather | solution.py:166
  202.6 7.0 fusion.74
  215.2 7.2 convolution_convert_fusion.1
  222.5 6.8 convolution_convert_fusion
  240.9 3.5 convolution_convert_fusion.4
  244.4 3.5 fusion.70
  247.9 5.7 convolution_convert_fusion.2
  253.7 66.5 %reduce-scatter.9.cloned.1.call-done = bf16[256,4096]{1,0:T(8,128)(2,1)} async-done(((bf16[1024,4096]{1,0:T(8,128)(2,1)}), bf16[256,4096]{1,0:T(8,128)(2,1)}) %reduce-scatter.9.cloned.1.call-update) | async-done | bytes 2097168 | tf_op jit(solution)/shard_map/reduce_scatter | solution.py:207
  320.2 74.0 %reduce-scatter.11.cloned.1.call-done = bf16[1024,1024]{1,0:T(8,128)(2,1)} async-done(((bf16[4096,1024]{1,0:T(8,128)(2,1)}), bf16[1024,1024]{1,0:T(8,128)(2,1)}) %reduce-scatter.11.cloned.1.call-update) | async-done | bytes 2097168 | tf_op jit(solution)/shard_map/reduce_scatter | solution.py:197
  394.3 61.3 %reduce-scatter.5.cloned.1.call-done = bf16[256,3072]{1,0:T(8,128)(2,1)} async-done(((bf16[1024,3072]{1,0:T(8,128)(2,1)}), bf16[256,3072]{1,0:T(8,128)(2,1)}) %reduce-scatter.5.cloned.1.call-update) | async-done | bytes 1572880 | tf_op jit(solution)/shard_map/reduce_scatter | solution.py:231
  455.7 5.1 all-gather.8
  463.8 7.2 fusion.37
  471.0 11.3 %all-reduce.11 = (bf16[1024]{0:T(1024)(128)(2,1)S(1)}, bf16[1024]{0:T(1024)(128)(2,1)S(1)}, bf16[1024]{0:T(1024)(128)(2,1)S(1)}, bf16[1024]{0:T(1024)(128)(2,1)S...) all-reduce(bf16[1024]{0:T(1024)(128)(2,1)S(1)} %get-tuple-element.1, ...), channel_id=3, replica_groups=mesh['replica'=8,'shard'=4] {'shard'}, use_global_device_ids=true, to_apply=%region_13.14.clone | all-reduce | flops 12288 | bytes 49152
  482.9 23.1 %all-reduce.9 = (bf16[256]{0:T(256)(128)(2,1)S(1)}, bf16[256]{0:T(256)(128)(2,1)S(1)}, bf16[256]{0:T(256)(128)(2,1)S(1)}, bf16[256]{0:T(256)(128)(2,1)S(1)}, bf1...) all-reduce(bf16[256]{0:T(256)(128)(2,1)S(1)} %dynamic-slice.1, ...), channel_id=1, replica_groups=mesh['replica'=8,'shard'=4] {'replica'}, use_global_device_ids=true, to_apply=%region_14.15 | all-reduce | flops 3072 | bytes 12288 | tf_op jit(solution)/shard_map/psum | solution.py:294
  513.1 5.6 fusion.17
  518.8 111.1 %all-reduce.14.cloned.1.call-done = (bf16[256,1024]{1,0:T(8,128)(2,1)}, bf16[256,4096]{1,0:T(8,128)(2,1)}, bf16[1024,1024]{1,0:T(8,128)(2,1)}) async-done(((bf16[256,1024]{1,0:T(8,128)(2,1)}, bf16[256,4096]{1,0:T(8,128)(2,1)}, bf16[1024,1024]{1,0:T(8,128)(2,1)}), (bf16[256,1024]{1,0:T(8,128)(2,1)}, bf16[256,4096]{1,0:T(8,128)(2,1)}, bf16[1024,1024]{1,0:T(8,128)(2,1)})) %all-reduce.14.cloned.1.call-update) | async-done | bytes 4718608 | tf_op jit(solution)/shard_map/psum | solution.py:299
  632.0 4.2 convert_element_type.250
  638.7 168.3 %all-gather.23.cloned.1.call-done = bf16[2048,3072]{1,0:T(8,128)(2,1)} async-done(((bf16[256,3072]{1,0:T(8,128)(2,1)}), bf16[2048,3072]{1,0:T(8,128)(2,1)}) %all-gather.23.cloned.1.call-update) | async-done | bytes 12582928 | tf_op jit(solution)/shard_map/all_gather | solution.py:296
  807.1 7.3 reduce_sum.208
  (141 shorter events, 40.9 us)
Async XLA Ops:
  7.2 51.6 %all-gather.15.cloned.1.call-start = ((), (), s32[]{:S(2)}) async-start(), calls=%async_computation.4 | async-start | bytes 7864320 | tf_op jit(solution)/shard_map/all_gather | solution.py:157
  7.9 75.1 %all-gather.17.cloned.1.call-start = ((), (), s32[]{:S(2)}) async-start(), calls=%async_computation.5 | async-start | bytes 2621440 | tf_op jit(solution)/shard_map/all_gather | solution.py:160
  8.7 7.5 copy-start.15
  8.7 12.9 %copy-start.16 = (bf16[256]{0:T(256)(128)(2,1)S(1)}, bf16[256]{0:T(256)(128)(2,1)}, u32[]{:S(2)}) copy-start(bf16[256]{0:T(256)(128)(2,1)} %param.19) | copy-start | bytes 1540
  8.7 18.1 %copy-start.17 = (bf16[256]{0:T(256)(128)(2,1)S(1)}, bf16[256]{0:T(256)(128)(2,1)}, u32[]{:S(2)}) copy-start(bf16[256]{0:T(256)(128)(2,1)} %param.22) | copy-start | bytes 1540
  8.7 23.3 %copy-start.18 = (bf16[256]{0:T(256)(128)(2,1)S(1)}, bf16[256]{0:T(256)(128)(2,1)}, u32[]{:S(2)}) copy-start(bf16[256]{0:T(256)(128)(2,1)} %param.23) | copy-start | bytes 1540
  8.7 28.5 %copy-start.13 = (bf16[1024]{0:T(1024)(128)(2,1)S(1)}, bf16[1024]{0:T(1024)(128)(2,1)}, u32[]{:S(2)}) copy-start(bf16[1024]{0:T(1024)(128)(2,1)} %param.29) | copy-start | bytes 6148
  8.7 33.9 %copy-start.19 = (bf16[256]{0:T(256)(128)(2,1)S(1)}, bf16[256]{0:T(256)(128)(2,1)}, u32[]{:S(2)}) copy-start(bf16[256]{0:T(256)(128)(2,1)} %param.27) | copy-start | bytes 1540
  8.7 39.1 %copy-start.20 = (bf16[256]{0:T(256)(128)(2,1)S(1)}, bf16[256]{0:T(256)(128)(2,1)}, u32[]{:S(2)}) copy-start(bf16[256]{0:T(256)(128)(2,1)} %param.26) | copy-start | bytes 1540
  8.7 44.3 %copy-start.21 = (s32[1,4]{1,0:T(1,128)S(1)}, s32[1,4]{1,0:T(1,128)}, u32[]{:S(2)}) copy-start(s32[1,4]{1,0:T(1,128)} %param.18) | copy-start | bytes 52
  8.8 44.6 %copy-start.1 = (bf16[128,1024]{1,0:T(8,128)(2,1)S(1)}, bf16[128,1024]{1,0:T(8,128)(2,1)}, u32[]{:S(2)}) copy-start(bf16[128,1024]{1,0:T(8,128)(2,1)} %param.16) | copy-start | bytes 786436
  8.8 134.1 %all-gather.19.cloned.1.call-start = ((), (), s32[]{:S(2)}) async-start(), calls=%async_computation.6 | async-start | bytes 10485760 | tf_op jit(solution)/shard_map/all_gather | solution.py:164
  9.5 193.0 %all-gather.21.cloned.1.call-start = ((), (), s32[]{:S(2)}) async-start(), calls=%async_computation.7 | async-start | bytes 10485760 | tf_op jit(solution)/shard_map/all_gather | solution.py:166
  10.1 243.6 %reduce-scatter.7.cloned.1.call-start = ((), (), s32[]{:S(2)}) async-start(), calls=%async_computation.9 | async-start | bytes 2621440 | tf_op jit(solution)/shard_map/reduce_scatter | solution.py:218
  63.2 21.9 %copy-start.10 = (bf16[128,1024]{0,1:T(8,128)(2,1)}, bf16[128,1024]{0,1:T(8,128)(2,1)S(1)}, u32[]{:S(2)}) copy-start(bf16[128,1024]{0,1:T(8,128)(2,1)S(1)} %copy.60) | copy-start | bytes 786436
  63.4 21.7 %copy-start.8 = (bf16[128,1024]{0,1:T(8,128)(2,1)}, bf16[128,1024]{0,1:T(8,128)(2,1)S(1)}, u32[]{:S(2)}) copy-start(bf16[128,1024]{0,1:T(8,128)(2,1)S(1)} %copy.61) | copy-start | bytes 786436
  63.8 19.2 %copy-start.7 = (f32[16,128,128]{1,2,0:T(8,128)}, f32[16,128,128]{1,2,0:T(8,128)S(1)}, u32[]{:S(2)}) copy-start(f32[16,128,128]{1,2,0:T(8,128)S(1)} %convolution_multiply_fusion.1) | copy-start | bytes 3145732
  64.3 78.6 %copy-start.11 = (bf16[16,64,128]{2,1,0:T(8,128)(2,1)}, bf16[16,64,128]{2,1,0:T(8,128)(2,1)S(1)}, u32[]{:S(2)}) copy-start(bf16[16,64,128]{2,1,0:T(8,128)(2,1)S(1)} %convolution_convert_fusion.6) | copy-start | bytes 786436
  142.8 59.7 %copy-start.4 = (bf16[128,1024]{1,0:T(8,128)(2,1)S(1)}, bf16[128,1024]{1,0:T(8,128)(2,1)}, u32[]{:S(2)}) copy-start(bf16[128,1024]{1,0:T(8,128)(2,1)} %param.17) | copy-start | bytes 786436
  202.5 7.1 copy-start
  209.6 3.1 copy-start.3
  209.6 3.1 copy-start.5
  209.6 3.3 copy-start.12
  215.0 105.2 %reduce-scatter.9.cloned.1.call-start = ((), (), s32[]{:S(2)}) async-start(), calls=%async_computation.10 | async-start | bytes 10485760 | tf_op jit(solution)/shard_map/reduce_scatter | solution.py:207
  222.5 171.7 %reduce-scatter.11.cloned.1.call-start = ((), (), s32[]{:S(2)}) async-start(), calls=%async_computation.11 | async-start | bytes 10485760 | tf_op jit(solution)/shard_map/reduce_scatter | solution.py:197
  229.3 226.3 %reduce-scatter.5.cloned.1.call-start = ((), (), s32[]{:S(2)}) async-start(), calls=%async_computation.8 | async-start | bytes 7864320 | tf_op jit(solution)/shard_map/reduce_scatter | solution.py:231
  229.4 3.0 copy-start.2
  253.6 376.3 %all-reduce.14.cloned.1.call-start = ((), (), s32[]{:S(2)}) async-start(), calls=%async_computation.13 | async-start | bytes 9437184 | tf_op jit(solution)/shard_map/psum | solution.py:299
  394.2 61.4 %copy-start.22 = (bf16[256]{0:T(256)(128)(2,1)S(1)}, bf16[256]{0:T(256)(128)(2,1)}, u32[]{:S(2)}) copy-start(bf16[256]{0:T(256)(128)(2,1)} %param.31) | copy-start | bytes 1540
  394.2 67.5 %copy-start.23 = (u32[32]{0:T(128)S(1)}, u32[32]{0:T(128)}, u32[]{:S(2)}) copy-start(u32[32]{0:T(128)} %constant.37) | copy-start | bytes 388
  394.2 412.8 %all-gather.23.cloned.1.call-start = ((), (), s32[]{:S(2)}) async-start(), calls=%async_computation.12 | async-start | bytes 14155776 | tf_op jit(solution)/shard_map/all_gather | solution.py:296
  632.0 4.3 copy-start.6
  (2 other events, 2.7 us)
Sparse Core Ops, SparseCore 0:
  9.6 49.2 all-gather.14
  60.4 22.5 all-gather.16
  84.5 58.2 all-gather.18
  144.2 58.2 all-gather.20
  215.1 31.1 reduce-scatter.6
  248.8 71.4 reduce-scatter.8
  322.8 71.3 reduce-scatter.10
  396.8 58.8 reduce-scatter.4
  459.6 170.2 all-reduce.13
  631.9 175.0 all-gather.22
